TPU v7x, 768 devices: a whole 4x8x12 slice. The times are simulated.
768 devices in a mesh: seq: 16 (over y, core), chan: 48 (over z, x).
Axes of the slice: x: 4, y: 8, z: 12, core: 2. Of those that a mesh axis runs over, the one named last changes fastest.
Arguments:
- queries: bfloat16 [48, 2048, 4096], P('chan', 'seq'), may hold values from -256 to 256
- keys: bfloat16 [48, 2048, 1024], P('chan', 'seq'), may hold values from -6 to 6
- values: bfloat16 [48, 2048, 1024], P('chan', 'seq'), may hold values from -6 to 6
- doc_lengths: int32 [48, 16], P('chan'), may hold values from 1 to 256, 2048 in all within a row
- rank_in: bfloat16 [4096, 256], replicated, may hold values from -0.09375 to 0.09375
- bc_weight: bfloat16 [4096, 32], replicated, may hold values from -0.09375 to 0.09375
- rank_out: bfloat16 [256, 4096], replicated, may hold values from -0.375 to 0.375
- dt_bias: float32 [4096], replicated, may hold values from -8 to -6
- a_log: float32 [4096, 16], replicated, may hold values from -10 to 4
- skip_gain: float32 [4096], replicated, may hold values from 0.5 to 1.5
Outputs:
- attn_out: bfloat16 [48, 2048, 4096], P('chan', 'seq')
- ssm_out: bfloat16 [48, 2048, 4096], P('chan', None, 'seq')
Inputs may be any that keep to these rules, and one draw needn't show every extreme that they name: `doc_lengths`: each row's entries are the lengths of its 16 documents in order and sum to 2048; some document of every row is 256 long.
All inputs are finite; a program needn't handle non-finite values.
Results may differ from a plain program's by a relative error of at most 0.0091.
Values may be sent and summed in bfloat16 or wider, within the bound.
A program may use at most 128 MiB of HBM per device.

v0:
```python
import functools
import math

import jax
import jax.numpy as jnp
from jax import lax
from jax.experimental import pallas as pl
from jax.experimental.pallas import tpu as pltpu
from jax.sharding import PartitionSpec as P

NS = 16
TOK = 128
SEGS = 16
PAR = 2
CW = 256
PACK = 160
ORDER = (1, 7, 2, 6, 0, 3, 5, 4)
LOG2E = 1.4426950408889634
MESH = pl.DeviceIdType.MESH
F32 = jnp.float32
BF16 = jnp.bfloat16
VMEM_LIMIT = 60 * 1024 * 1024


def dot(a, b, ca=1, cb=0):
    return lax.dot_general(a, b, (((ca,), (cb,)), ((), ())), preferred_element_type=F32)


def softplus(v):
    z = jnp.exp(-jnp.abs(v))
    series = z * (1.0 - z * (0.5 - z * (1.0 / 3.0 - z * 0.25)))
    return jnp.maximum(v, 0.0) + jnp.where(z < 0.03125, series, jnp.log(1.0 + z))


def attend_kernel(
    doc, q_hbm, k_hbm, v_hbm, rin_hbm, bcw_hbm,
    attn_hbm, xr_hbm, pk,
    qb, kb, vb, wb, bb, ab, po,
    loc_sem, kv_send, kv_recv, x_send, x_recv, p_send, p_recv,
):
    s = lax.axis_index("seq")
    y = lax.div(s, 2)
    c = lax.rem(s, 2)
    sib = s + 1 - 2 * c

    def local(src, dst, i):
        return pltpu.make_async_copy(src, dst, loc_sem.at[i])

    def remote(src, dst, send, recv, to):
        return pltpu.make_async_remote_copy(
            src_ref=src, dst_ref=dst, send_sem=send, recv_sem=recv,
            device_id={"seq": to}, device_id_type=MESH,
        )

    loads = [
        local(k_hbm.at[0], kb.at[0], 0),
        local(q_hbm.at[0], qb, 1),
        local(v_hbm.at[0], vb.at[0], 2),
        local(rin_hbm, wb, 3),
        local(bcw_hbm, bb, 4),
    ]
    barrier = pltpu.get_barrier_semaphore()
    for d in range(1, 16):
        pl.semaphore_signal(
            barrier, inc=1, device_id={"seq": lax.rem(s + d, 16)}, device_id_type=MESH
        )
    for one in loads:
        one.start()

    @pl.when(s < 1)
    def _():
        kb[1] = jnp.zeros_like(kb[1])
        vb[1] = jnp.zeros_like(vb[1])

    @pl.when(s < 2)
    def _():
        kb[2] = jnp.zeros_like(kb[2])
        vb[2] = jnp.zeros_like(vb[2])

    first = s * TOK
    qpos = first + lax.broadcasted_iota(jnp.int32, (TOK, TOK), 0)
    lane = lax.broadcasted_iota(jnp.int32, (TOK, TOK), 1)
    begin = jnp.zeros((TOK, TOK), jnp.int32)
    bound = jnp.int32(0)
    for j in range(16):
        bound = bound + doc[0, j]
        begin = jnp.where(qpos >= bound, bound, begin)
    masks = []
    for b in range(3):
        kpos = first - b * TOK + lane
        masks.append((kpos <= qpos) & (kpos >= begin))

    pl.semaphore_wait(barrier, 15)

    k_own, v_own = k_hbm.at[0], v_hbm.at[0]
    to1 = lax.rem(s + 1, 16)
    to2 = lax.rem(s + 2, 16)
    send1 = [remote(o, d.at[1], kv_send.at[0, i], kv_recv.at[0, i], to1)
             for i, (o, d) in enumerate(((k_own, kb), (v_own, vb)))]
    send2 = [remote(o, d.at[2], kv_send.at[1, i], kv_recv.at[1, i], to2)
             for i, (o, d) in enumerate(((k_own, kb), (v_own, vb)))]
    pass2 = [remote(d.at[1], d.at[2], kv_send.at[2, i], kv_recv.at[1, i], sib)
             for i, d in enumerate((kb, vb))]
    for i in range(2):
        @pl.when(s < 15)
        def _():
            send1[i].start()

        @pl.when((c == 0) & (s < 14))
        def _():
            send2[i].start()

    for i in range(2):
        @pl.when(s >= 1)
        def _():
            send1[i].wait_recv()

        @pl.when((c == 0) & (s >= 2))
        def _():
            pass2[i].start()

    for one in loads[:3]:
        one.wait()
    for i in range(2):
        @pl.when(s >= 2)
        def _():
            send2[i].wait_recv()

    def send_tiles(g):
        for cc in range(2):
            to = 2 * g + cc
            cols = pl.ds(pl.multiple_of(to * CW, CW), CW)
            here = pl.ds(pl.multiple_of(s * TOK, TOK), TOK)

            @pl.when(to != s)
            def _():
                remote(ab.at[:, cols], xr_hbm.at[here], x_send.at[to], x_recv.at[s], to).start()

            @pl.when(to == s)
            def _():
                local(ab.at[:, cols], xr_hbm.at[here], 5).start()

    def group(i):
        off = jnp.int32(0)
        for at, value in enumerate(ORDER):
            off = jnp.where(i == at, value, off)
        return lax.rem(y + off, 8)

    scale = LOG2E / math.sqrt(128.0)

    def step(i, _):
        g = group(i)
        qcols = pl.ds(pl.multiple_of(g * 512, 512), 512)
        kcols = pl.ds(pl.multiple_of(g * 128, 128), 128)
        keys = [kb[b, :, kcols] for b in range(3)]
        vals = [vb[b, :, kcols] for b in range(3)]
        for j in range(4):
            hcols = pl.ds(pl.multiple_of(g * 512 + j * 128, 128), 128)
            q = qb[:, hcols]
            t = [jnp.where(masks[b], dot(q, keys[b], 1, 1) * scale, -1e30) for b in range(3)]
            top = jnp.max(jnp.maximum(jnp.maximum(t[0], t[1]), t[2]), axis=1, keepdims=True)
            e = [jnp.exp2(one - top) for one in t]
            inv = 1.0 / jnp.sum(e[0] + e[1] + e[2], axis=1, keepdims=True)
            o = dot((e[0] * inv).astype(BF16), vals[0])
            o = o + dot((e[1] * inv).astype(BF16), vals[1])
            o = o + dot((e[2] * inv).astype(BF16), vals[2])
            ab[:, hcols] = o.astype(BF16)

        @pl.when((i > 0) & (i < 6))
        def _():
            send_tiles(group(i - 1))

        return 0

    lax.fori_loop(0, 8, step, 0)
    out_copy = local(ab, attn_hbm.at[0], 6)
    out_copy.start()

    loads[3].wait()
    loads[4].wait()
    x = ab[...]
    po[pl.ds(0, TOK), :] = dot(x, wb[...]).astype(BF16)
    bct = dot(bb[...], x, 1, 1)
    po[pl.ds(TOK, 2 * NS), :] = jnp.concatenate([bct, bct], axis=1).astype(BF16)

    own = local(po, pk.at[s], 7)
    own.start()

    def slot(chip, core):
        return 2 * lax.rem(chip + 8, 8) + core

    right = slot(y + 1, c)
    left = slot(y - 1, c)
    ring = {}
    across = {}
    across[0] = remote(po, pk.at[s], p_send.at[7], p_recv.at[s], sib)
    ring[("r", 0)] = remote(po, pk.at[s], p_send.at[0], p_recv.at[s], right)
    ring[("l", 0)] = remote(po, pk.at[s], p_send.at[4], p_recv.at[s], left)
    ring[("r", 0)].start()
    ring[("l", 0)].start()
    across[0].start()
    send_tiles(group(5))

    def arrived(at):
        remote(po, pk.at[at], p_send.at[0], p_recv.at[at], sib).wait_recv()

    for k in range(1, 5):
        at = slot(y - k, c)
        arrived(at)
        if k < 4:
            ring[("r", k)] = remote(pk.at[at], pk.at[at], p_send.at[k], p_recv.at[at], right)
            ring[("r", k)].start()
        across[k] = remote(pk.at[at], pk.at[at], p_send.at[7 + k], p_recv.at[at], sib)
        across[k].start()
        if k < 4:
            at = slot(y + k, c)
            arrived(at)
            if k < 3:
                ring[("l", k)] = remote(pk.at[at], pk.at[at], p_send.at[4 + k], p_recv.at[at], left)
                ring[("l", k)].start()
            across[-k] = remote(pk.at[at], pk.at[at], p_send.at[11 + k], p_recv.at[at], sib)
            across[-k].start()
        if k < 3:
            send_tiles(group(5 + k))

    for k in range(-3, 5):
        arrived(slot(y + k, 1 - c))
    own.wait()
    out_copy.wait()
    for one in list(ring.values()) + list(across.values()):
        one.wait_send()
    for i in range(2):
        @pl.when(s < 15)
        def _():
            send1[i].wait_send()

        @pl.when((c == 0) & (s < 14))
        def _():
            send2[i].wait_send()

        @pl.when((c == 0) & (s >= 2))
        def _():
            pass2[i].wait_send()
    local(ab.at[:, pl.ds(0, CW)], xr_hbm.at[pl.ds(0, TOK)], 5).wait()
    for d in range(1, 16):
        frm = lax.rem(s + d, 16)
        one = remote(
            ab.at[:, pl.ds(0, CW)], xr_hbm.at[pl.ds(0, TOK)], x_send.at[frm], x_recv.at[frm], frm
        )
        one.wait_send()
        one.wait_recv()


def attend(doc, queries, keys, values, rank_in, bc_weight):
    anyspace = pl.BlockSpec(memory_space=pl.ANY)
    return pl.pallas_call(
        attend_kernel,
        out_shape=(
            jax.ShapeDtypeStruct((1, TOK, 4096), BF16),
            jax.ShapeDtypeStruct((SEGS * TOK, CW), BF16),
            jax.ShapeDtypeStruct((SEGS, PACK, CW), BF16),
        ),
        in_specs=[pl.BlockSpec(memory_space=pltpu.SMEM)] + [anyspace] * 5,
        out_specs=(anyspace, anyspace, pl.BlockSpec(memory_space=pltpu.VMEM)),
        scratch_shapes=[
            pltpu.VMEM((TOK, 4096), BF16),
            pltpu.VMEM((3, TOK, 1024), BF16),
            pltpu.VMEM((3, TOK, 1024), BF16),
            pltpu.VMEM((4096, 256), BF16),
            pltpu.VMEM((2 * NS, 4096), BF16),
            pltpu.VMEM((TOK, 4096), BF16),
            pltpu.VMEM((PACK, CW), BF16),
            pltpu.SemaphoreType.DMA((8,)),
            pltpu.SemaphoreType.DMA((3, 2)),
            pltpu.SemaphoreType.DMA((2, 2)),
            pltpu.SemaphoreType.DMA((16,)),
            pltpu.SemaphoreType.DMA((16,)),
            pltpu.SemaphoreType.DMA((15,)),
            pltpu.SemaphoreType.DMA((16,)),
        ],
        compiler_params=pltpu.CompilerParams(
            collective_id=0, has_side_effects=True, vmem_limit_bytes=VMEM_LIMIT
        ),
        name="attend",
    )(doc, queries, keys, values, rank_in, bc_weight)


def scan_kernel(
    x, pk, rout_hbm, bias_hbm, alog_hbm, skip_hbm,
    out,
    dt, u, cum, cb, yl, pre, ha, hc, rw, bias, al, skip, bt, tot, pay, grp, xbuf, zbuf,
    loc_sem, xs_sem, xr_sem, zs_sem, zr_sem,
):
    s = lax.axis_index("seq")
    r = lax.axis_index("chan")
    zi = lax.div(r, 4)
    xi = lax.rem(r, 4)
    at = pl.multiple_of(s * CW, CW)
    loads = [
        pltpu.make_async_copy(rout_hbm.at[:, pl.ds(at, CW)], rw, loc_sem.at[0]),
        pltpu.make_async_copy(bias_hbm.at[:, pl.ds(at, CW)], bias, loc_sem.at[1]),
        pltpu.make_async_copy(alog_hbm.at[:, pl.ds(at, CW)], al, loc_sem.at[2]),
        pltpu.make_async_copy(skip_hbm.at[:, pl.ds(at, CW)], skip, loc_sem.at[3]),
    ]
    for one in loads:
        one.start()
    zbuf[...] = jnp.zeros_like(zbuf)
    xbuf[...] = jnp.zeros_like(xbuf)
    ha[...] = jnp.zeros_like(ha)
    hc[...] = jnp.zeros_like(hc)

    barrier = pltpu.get_barrier_semaphore()

    def chan(zz, xx):
        return 4 * lax.rem(zz + 12, 12) + lax.rem(xx + 4, 4)

    for d in range(1, 4):
        pl.semaphore_signal(barrier, inc=1, device_id={"chan": chan(zi, xi + d)}, device_id_type=MESH)
    for d in range(1, 12):
        pl.semaphore_signal(barrier, inc=1, device_id={"chan": chan(zi + d, xi)}, device_id_type=MESH)
    for one in loads:
        one.wait()

    rate = -jnp.exp(al[...]) * LOG2E
    rates = (rate[:8], rate[8:])

    row = lax.broadcasted_iota(jnp.int32, (TOK, TOK), 0)
    col = lax.broadcasted_iota(jnp.int32, (TOK, TOK), 1)
    tri = (col <= row).astype(BF16)
    spread = (lax.rem(lax.broadcasted_iota(jnp.int32, (NS, CW), 1), NS)
              == lax.broadcasted_iota(jnp.int32, (NS, CW), 0)).astype(BF16)
    block = (lax.div(lax.broadcasted_iota(jnp.int32, (TOK, CW), 1), NS)
             == lax.rem(lax.broadcasted_iota(jnp.int32, (TOK, CW), 0), NS))

    def prepare(q, _):
        for j in range(4):
            seg = q * 4 + j
            rows = pl.ds(pl.multiple_of(seg * TOK, TOK), TOK)
            low = pk[seg, pl.ds(0, TOK), :]
            step = softplus(dot(low, rw[...]) + bias[...])
            dt[rows, :] = step
            u[rows, :] = step * x[rows, :].astype(F32)
            hi = step.astype(BF16)
            lo = (step - hi.astype(F32)).astype(BF16)
            run = dot(tri, hi) + dot(tri, lo)
            cum[rows, :] = run
            tot[pl.ds(seg, 1), :] = run[TOK - 1:, :]
            maps = pk[seg, pl.ds(TOK, 2 * NS), pl.ds(0, TOK)]
            bt[pl.ds(pl.multiple_of(seg * NS, NS), NS), :] = maps[:NS].astype(F32)
            wide_c = dot(maps[NS:], spread, 0, 0)
            cb[rows, :] = jnp.where(block, wide_c, 0.0).astype(BF16)
        return 0

    lax.fori_loop(0, SEGS // 4, prepare, 0)

    def rows_of(seg, chunk):
        return pl.ds(pl.multiple_of(seg * TOK + chunk * 16, 16), 16)

    def pair(p, _):
        def body(q, carry):
            states, maps = carry
            states = [list(one) for one in states]
            for half, (held, ready) in enumerate(((ha, hc), (hc, ha))):
                for k in range(PAR):
                    if half == 0:
                        wrapped = q == 0
                        seg = jnp.where(wrapped, lax.rem(p + 7, 8), p) * PAR + k
                        done = rows_of(seg, jnp.where(wrapped, 7, 2 * q - 1))
                    else:
                        done = rows_of(p * PAR + k, 2 * q)
                    yl[done, :] = dot(cb[done, :], ready[k])
                for t in range(16):
                    for k in range(PAR):
                        at_row = (p * PAR + k) * TOK + (2 * q + half) * 16 + t
                        d = jnp.broadcast_to(dt[pl.ds(at_row, 1), :], (8, CW))
                        w = jnp.broadcast_to(u[pl.ds(at_row, 1), :], (8, CW))
                        lane = half * 16 + t
                        for h in range(2):
                            b = jnp.broadcast_to(maps[k][8 * h: 8 * h + 8, lane: lane + 1], (8, TOK))
                            b = jnp.concatenate([b, b], axis=1)
                            states[k][h] = jnp.exp2(d * rates[h]) * states[k][h] + w * b
                        held[k, pl.ds(16 * t, 16), :] = jnp.concatenate(states[k], axis=0).astype(BF16)
            maps = tuple(pltpu.roll(one, TOK - 32, axis=1) for one in maps)
            return tuple(tuple(one) for one in states), maps

        zero = jnp.zeros((8, CW), F32)
        maps = tuple(
            bt[pl.ds(pl.multiple_of((p * PAR + k) * NS, NS), NS), :] for k in range(PAR)
        )
        states, _ = lax.fori_loop(0, 4, body, (((zero, zero),) * PAR, maps))
        for k in range(PAR):
            pre[p * PAR + k] = jnp.concatenate(states[k], axis=0)
        return 0

    lax.fori_loop(0, SEGS // PAR, pair, 0)
    for k in range(PAR):
        done = rows_of(SEGS - PAR + k, 7)
        yl[done, :] = dot(cb[done, :], hc[k])

    state = jnp.zeros((NS, CW), F32)
    total = jnp.zeros((1, CW), F32)
    for seg in range(SEGS):
        mine = pre[seg]
        t = tot[pl.ds(seg, 1), :]
        pre[seg] = state
        state = jnp.exp2(rate * t) * state + mine
        total = total + t
    pay[pl.ds(0, NS), :] = state
    pay[pl.ds(NS, 8), :] = jnp.broadcast_to(total, (8, CW))
    pl.semaphore_wait(barrier, 14)

    sends = []
    for d in range(1, 4):
        sends.append(pltpu.make_async_remote_copy(
            src_ref=pay, dst_ref=xbuf.at[xi], send_sem=xs_sem.at[d - 1], recv_sem=xr_sem.at[xi],
            device_id={"chan": chan(zi, xi + d)}, device_id_type=MESH))
    for one in sends:
        one.start()
    for d in range(1, 4):
        frm = lax.rem(xi + d, 4)
        pltpu.make_async_remote_copy(
            src_ref=pay, dst_ref=xbuf.at[frm], send_sem=xs_sem.at[d - 1], recv_sem=xr_sem.at[frm],
            device_id={"chan": chan(zi, frm)}, device_id_type=MESH).wait_recv()
    gs = jnp.zeros((NS, CW), F32)
    gt = jnp.zeros((1, CW), F32)
    ms = jnp.zeros((NS, CW), F32)
    mt = jnp.zeros((1, CW), F32)
    own = pay[...]
    for i in range(4):
        got = jnp.where(xi == i, own, xbuf[i])
        os, ot = got[:NS], got[NS: NS + 1]
        dec = jnp.exp2(rate * ot)
        gs = dec * gs + os
        gt = gt + ot
        ms = jnp.where(i < xi, gs, ms)
        mt = jnp.where(i < xi, gt, mt)
    grp[pl.ds(0, NS), :] = gs
    grp[pl.ds(NS, 8), :] = jnp.broadcast_to(gt, (8, CW))

    def zcopy(d, slot):
        return pltpu.make_async_remote_copy(
            src_ref=grp, dst_ref=zbuf.at[slot], send_sem=zs_sem.at[d], recv_sem=zr_sem.at[slot],
            device_id={"chan": chan(zi + d, xi)}, device_id_type=MESH)

    for d in range(11, 0, -1):
        @pl.when(zi + d < 12)
        def _():
            zcopy(d, zi).start()
    for d in range(1, 12):
        @pl.when(zi - d >= 0)
        def _():
            zcopy(d, lax.rem(zi - d + 12, 12)).wait_recv()
    zs = jnp.zeros((NS, CW), F32)
    for i in range(11):
        got = zbuf[i]
        new = jnp.exp2(rate * got[NS: NS + 1]) * zs + got[:NS]
        zs = jnp.where(i < zi, new, zs)
    row_in = jnp.exp2(rate * mt) * zs + ms
    done = jnp.zeros((1, CW), F32)
    for seg in range(SEGS):
        pre[seg] = pre[seg] + jnp.exp2(rate * done) * row_in
        done = done + tot[pl.ds(seg, 1), :]

    def write(rows, ready):
        got = yl[rows, :] + dot(cb[rows, :], ready)
        out[0, rows, :] = (got + skip[...] * x[rows, :].astype(F32)).astype(BF16)

    def carried(q, _):
        seg = lax.div(q, 4)
        start = pre[seg]
        starts = (start[:8], start[8:])
        for half, (held, ready) in enumerate(((ha, hc), (hc, ha))):
            if half == 0:
                before = jnp.where(q == 0, SEGS * TOK - 16, 32 * q - 16)
            else:
                before = 32 * q
            write(pl.ds(pl.multiple_of(before, 16), 16), ready[0])
            for t in range(16):
                d = jnp.broadcast_to(cum[pl.ds(32 * q + 16 * half + t, 1), :], (8, CW))
                g = [jnp.exp2(d * rates[h]) * starts[h] for h in range(2)]
                held[0, pl.ds(16 * t, 16), :] = jnp.concatenate(g, axis=0).astype(BF16)
        return 0

    lax.fori_loop(0, SEGS * TOK // 32, carried, 0)
    write(pl.ds(SEGS * TOK - 16, 16), hc[0])
    for one in sends:
        one.wait_send()
    for d in range(1, 12):
        @pl.when(zi + d < 12)
        def _():
            zcopy(d, zi).wait_send()


def scan(x, pk, rank_out, dt_bias, a_log, skip_gain):
    anyspace = pl.BlockSpec(memory_space=pl.ANY)
    vm = pl.BlockSpec(memory_space=pltpu.VMEM)
    rows = SEGS * TOK
    return pl.pallas_call(
        scan_kernel,
        out_shape=jax.ShapeDtypeStruct((1, rows, CW), BF16),
        in_specs=[vm, vm] + [anyspace] * 4,
        out_specs=vm,
        scratch_shapes=[
            pltpu.VMEM((rows, CW), F32),
            pltpu.VMEM((rows, CW), F32),
            pltpu.VMEM((rows, CW), F32),
            pltpu.VMEM((rows, CW), BF16),
            pltpu.VMEM((rows, CW), F32),
            pltpu.VMEM((SEGS, NS, CW), F32),
            pltpu.VMEM((PAR, 256, CW), BF16),
            pltpu.VMEM((PAR, 256, CW), BF16),
            pltpu.VMEM((256, CW), BF16),
            pltpu.VMEM((1, CW), F32),
            pltpu.VMEM((NS, CW), F32),
            pltpu.VMEM((1, CW), F32),
            pltpu.VMEM((SEGS * NS, TOK), F32),
            pltpu.VMEM((SEGS, CW), F32),
            pltpu.VMEM((24, CW), F32),
            pltpu.VMEM((24, CW), F32),
            pltpu.VMEM((4, 24, CW), F32),
            pltpu.VMEM((12, 24, CW), F32),
            pltpu.SemaphoreType.DMA((4,)),
            pltpu.SemaphoreType.DMA((3,)),
            pltpu.SemaphoreType.DMA((4,)),
            pltpu.SemaphoreType.DMA((12,)),
            pltpu.SemaphoreType.DMA((12,)),
        ],
        compiler_params=pltpu.CompilerParams(
            collective_id=1, has_side_effects=True, vmem_limit_bytes=VMEM_LIMIT
        ),
        name="scan",
    )(x, pk, rank_out, dt_bias, a_log, skip_gain)


def local(
    queries, keys, values, doc_lengths, rank_in, bc_weight, rank_out, dt_bias, a_log, skip_gain
):
    attn_out, x, pk = attend(doc_lengths, queries, keys, values, rank_in, bc_weight.T)
    ssm_out = scan(x, pk, rank_out, dt_bias[None], a_log.T, skip_gain[None])
    return (attn_out, ssm_out)


def solution(mesh):
    return jax.shard_map(
        local,
        mesh=mesh,
        in_specs=(
            P("chan", "seq", None),
            P("chan", "seq", None),
            P("chan", "seq", None),
            P("chan", None),
            P(),
            P(),
            P(),
            P(),
            P(),
            P(),
        ),
        out_specs=(P("chan", "seq", None), P("chan", None, "seq")),
        check_vma=False,
    )
```

profile of v0, /device:TPU:513, one launch (start us, length us, event | category | flops | bytes accessed | tf_op | source)
XLA Modules:
  0.0 112.1 jit_solution(17931968832855097276)
XLA Ops:
  0.6 63.4 %attend.1 = (bf16[1,128,4096]{2,1,0:T(8,128)(2,1)}, bf16[2048,256]{1,0:T(8,128)(2,1)}, bf16[16,160,256]{2,1,0:T(8,128)(2,1)}) custom-call(s32[1,16]{1,0:T(1,128)} %doc.1, bf16[1,128,4096]{2,1,0:T(8,128)(2,1)} %q_hbm.1, bf16[1,128,1024]{2,1,0:T(8,128)(2,1)} %k_hbm.1, bf16[1,128,1024]{2,1,0:T(8,128)(2,1)} %v_hbm.1, bf16[4096,256]{1,0:T(8,128)(2,1)} %rin_hbm.1, ...), custom_call_target="tpu_custom_call" | custom-call | tf_op jit(solution)/shard_map/attend/pallas_call | solution.py:256
  64.1 0.0 copy-start.1
  64.1 45.5 %scan.1 = bf16[1,2048,256]{2,1,0:T(8,128)(2,1)} custom-call(bf16[2048,256]{1,0:T(8,128)(2,1)} %get-tuple-element.6.x, bf16[16,160,256]{2,1,0:T(8,128)(2,1)} %get-tuple-element.7.pk, bf16[256,4096]{1,0:T(8,128)(2,1)} %rout_hbm.1, f32[1,4096]{1,0:T(1,128)} %bitcast.6, f32[16,4096]{1,0:T(8,128)} %bitcast.5, f32[1,4096]{1,0:T(1,128)} %bitcast.7), custom_call_target="tpu_custom_call" | custom-call | tf_op jit(solution)/shard_map/scan/pallas_call | solution.py:498
  109.6 0.0 copy-done.1
  109.6 0.0 copy-start
  109.6 1.0 copy.14
  110.6 0.6 copy-done
  111.2 1.0 copy.15
Async XLA Ops:
  64.1 45.5 %copy-start.1 = (bf16[1,128,4096]{2,1,0:T(8,128)(2,1)S(1)}, bf16[1,128,4096]{2,1,0:T(8,128)(2,1)}, u32[]{:S(2)}) copy-start(bf16[1,128,4096]{2,1,0:T(8,128)(2,1)} %get-tuple-element.10) | copy-start | bytes 3145732
  109.6 1.6 %copy-start = (bf16[1,2048,256]{2,1,0:T(8,128)(2,1)S(1)}, bf16[1,2048,256]{2,1,0:T(8,128)(2,1)}, u32[]{:S(2)}) copy-start(bf16[1,2048,256]{2,1,0:T(8,128)(2,1)} %scan.1) | copy-start | bytes 3145732
where the time goes:
time: 112 us
  Pallas kernels  109 us (97%)
  local copies, waits for them, and re-layouts  2.57 us (2%)
    pallas_call x1, Pallas kernels, attend(): pl.pallas_call(attend_kernel, out_shape=(jax.ShapeDtypeStruct((1, TOK, 40...  63.4 us
    pallas_call x1, Pallas kernels, scan(): pl.pallas_call(scan_kernel, out_shape=jax.ShapeDtypeStruct((1, rows, CW),...  45.5 us
    unnamed x6, local copies, waits for them, and re-layouts  2.57 us

commit v1 on v0

--- a/solution.py
+++ b/solution.py
@@ -14,7 +14,7 @@
 PAR = 2
 CW = 256
 PACK = 160
-ORDER = (1, 7, 2, 6, 0, 3, 5, 4)
+ORDER = (7, 6, 1, 2, 5, 0, 3, 4)
 LOG2E = 1.4426950408889634
 MESH = pl.DeviceIdType.MESH
 F32 = jnp.float32
@@ -35,8 +35,8 @@
 def attend_kernel(
     doc, q_hbm, k_hbm, v_hbm, rin_hbm, bcw_hbm,
     attn_hbm, xr_hbm, pk,
-    qb, kb, vb, wb, bb, ab, po,
-    loc_sem, kv_send, kv_recv, x_send, x_recv, p_send, p_recv,
+    qb, kb, vb, wb, bb, ab, po, rb,
+    loc_sem, kv_send, kv_recv, x_send, x_recv, p_send, p_recv, r_send, r_recv, f_send,
 ):
     s = lax.axis_index("seq")
     y = lax.div(s, 2)
@@ -92,39 +92,66 @@
 
     pl.semaphore_wait(barrier, 15)
 
-    k_own, v_own = k_hbm.at[0], v_hbm.at[0]
+    def group(chip, i):
+        off = jnp.int32(0)
+        for at, value in enumerate(ORDER):
+            off = jnp.where(i == at, value, off)
+        return lax.rem(chip + off, 8)
+
     to1 = lax.rem(s + 1, 16)
     to2 = lax.rem(s + 2, 16)
-    send1 = [remote(o, d.at[1], kv_send.at[0, i], kv_recv.at[0, i], to1)
-             for i, (o, d) in enumerate(((k_own, kb), (v_own, vb)))]
-    send2 = [remote(o, d.at[2], kv_send.at[1, i], kv_recv.at[1, i], to2)
-             for i, (o, d) in enumerate(((k_own, kb), (v_own, vb)))]
-    pass2 = [remote(d.at[1], d.at[2], kv_send.at[2, i], kv_recv.at[1, i], sib)
-             for i, d in enumerate((kb, vb))]
-    for i in range(2):
-        @pl.when(s < 15)
-        def _():
-            send1[i].start()
-
-        @pl.when((c == 0) & (s < 14))
-        def _():
-            send2[i].start()
-
-    for i in range(2):
-        @pl.when(s >= 1)
-        def _():
-            send1[i].wait_recv()
-
-        @pl.when((c == 0) & (s >= 2))
-        def _():
-            pass2[i].start()
+    both = ((k_hbm.at[0], kb), (v_hbm.at[0], vb))
+
+    def head(chip, i):
+        return pl.ds(pl.multiple_of(group(chip, i) * 128, 128), 128)
+
+    def send1(i):
+        cols = head(lax.div(to1, 2), i)
+        return [remote(o.at[:, cols], d.at[1, :, cols], kv_send.at[0, i, n], kv_recv.at[0, i, n], to1)
+                for n, (o, d) in enumerate(both)]
+
+    def send2(i):
+        cols = head(lax.div(to2, 2), i)
+        return [remote(o.at[:, cols], d.at[2, :, cols], kv_send.at[1, i, n], kv_recv.at[1, i, n], to2)
+                for n, (o, d) in enumerate(both)]
+
+    def pass2(i):
+        cols = head(y, i)
+        return [remote(d.at[1, :, cols], d.at[2, :, cols], kv_send.at[2, i, n], kv_recv.at[1, i, n], sib)
+                for n, (o, d) in enumerate(both)]
+
+    def start_kv(i, _):
+        for n in range(2):
+            @pl.when(s < 15)
+            def _():
+                send1(i)[n].start()
+
+            @pl.when((c == 0) & (s < 14))
+            def _():
+                send2(i)[n].start()
+
+        return 0
+
+    lax.fori_loop(0, 8, start_kv, 0)
+
+    def arrive_kv(i):
+        cols = head(y, i)
+        for n, (o, d) in enumerate(both):
+            @pl.when(s >= 1)
+            def _():
+                remote(d.at[0, :, cols], d.at[1, :, cols], kv_send.at[0, i, n], kv_recv.at[0, i, n], sib).wait_recv()
+
+            @pl.when((c == 0) & (s >= 2))
+            def _():
+                pass2(i)[n].start()
+
+        for n, (o, d) in enumerate(both):
+            @pl.when(s >= 2)
+            def _():
+                remote(d.at[0, :, cols], d.at[2, :, cols], kv_send.at[1, i, n], kv_recv.at[1, i, n], sib).wait_recv()
 
     for one in loads[:3]:
         one.wait()
-    for i in range(2):
-        @pl.when(s >= 2)
-        def _():
-            send2[i].wait_recv()
 
     def send_tiles(g):
         for cc in range(2):
@@ -140,16 +167,11 @@
             def _():
                 local(ab.at[:, cols], xr_hbm.at[here], 5).start()
 
-    def group(i):
-        off = jnp.int32(0)
-        for at, value in enumerate(ORDER):
-            off = jnp.where(i == at, value, off)
-        return lax.rem(y + off, 8)
-
     scale = LOG2E / math.sqrt(128.0)
 
     def step(i, _):
-        g = group(i)
+        arrive_kv(i)
+        g = group(y, i)
         qcols = pl.ds(pl.multiple_of(g * 512, 512), 512)
         kcols = pl.ds(pl.multiple_of(g * 128, 128), 128)
         keys = [kb[b, :, kcols] for b in range(3)]
@@ -166,9 +188,9 @@
             o = o + dot((e[2] * inv).astype(BF16), vals[2])
             ab[:, hcols] = o.astype(BF16)
 
-        @pl.when((i > 0) & (i < 6))
+        @pl.when((i > 0) & (i < 7))
         def _():
-            send_tiles(group(i - 1))
+            send_tiles(group(y, i - 1))
 
         return 0
 
@@ -199,7 +221,20 @@
     ring[("r", 0)].start()
     ring[("l", 0)].start()
     across[0].start()
-    send_tiles(group(5))
+
+    def relay(cc):
+        to = 2 * lax.rem(y + 4, 8) + cc
+        cols = pl.ds(pl.multiple_of(to * CW, CW), CW)
+        return remote(ab.at[:, cols], rb.at[cc], r_send.at[cc], r_recv.at[cc], left)
+
+    def forward(cc):
+        frm = slot(y + 1, c)
+        here = pl.ds(pl.multiple_of(frm * TOK, TOK), TOK)
+        to = 2 * lax.rem(y + 5, 8) + cc
+        return remote(rb.at[cc], xr_hbm.at[here], f_send.at[cc], x_recv.at[frm], to)
+
+    for cc in range(2):
+        relay(cc).start()
 
     def arrived(at):
         remote(po, pk.at[at], p_send.at[0], p_recv.at[at], sib).wait_recv()
@@ -220,8 +255,11 @@
                 ring[("l", k)].start()
             across[-k] = remote(pk.at[at], pk.at[at], p_send.at[11 + k], p_recv.at[at], sib)
             across[-k].start()
-        if k < 3:
-            send_tiles(group(5 + k))
+        if k == 1:
+            send_tiles(group(y, 6))
+            for cc in range(2):
+                relay(cc).wait_recv()
+                forward(cc).start()
 
     for k in range(-3, 5):
         arrived(slot(y + k, 1 - c))
@@ -229,26 +267,38 @@
     out_copy.wait()
     for one in list(ring.values()) + list(across.values()):
         one.wait_send()
-    for i in range(2):
-        @pl.when(s < 15)
-        def _():
-            send1[i].wait_send()
-
-        @pl.when((c == 0) & (s < 14))
-        def _():
-            send2[i].wait_send()
-
-        @pl.when((c == 0) & (s >= 2))
-        def _():
-            pass2[i].wait_send()
+    for cc in range(2):
+        relay(cc).wait_send()
+        forward(cc).wait_send()
+
+    def end_kv(i, _):
+        for n in range(2):
+            @pl.when(s < 15)
+            def _():
+                send1(i)[n].wait_send()
+
+            @pl.when((c == 0) & (s < 14))
+            def _():
+                send2(i)[n].wait_send()
+
+            @pl.when((c == 0) & (s >= 2))
+            def _():
+                pass2(i)[n].wait_send()
+
+        return 0
+
+    lax.fori_loop(0, 8, end_kv, 0)
     local(ab.at[:, pl.ds(0, CW)], xr_hbm.at[pl.ds(0, TOK)], 5).wait()
     for d in range(1, 16):
         frm = lax.rem(s + d, 16)
         one = remote(
             ab.at[:, pl.ds(0, CW)], xr_hbm.at[pl.ds(0, TOK)], x_send.at[frm], x_recv.at[frm], frm
         )
-        one.wait_send()
         one.wait_recv()
+
+        @pl.when(lax.rem(lax.div(frm, 2) + 8 - y, 8) != 4)
+        def _():
+            one.wait_send()
 
 
 def attend(doc, queries, keys, values, rank_in, bc_weight):
@@ -270,13 +320,17 @@
             pltpu.VMEM((2 * NS, 4096), BF16),
             pltpu.VMEM((TOK, 4096), BF16),
             pltpu.VMEM((PACK, CW), BF16),
+            pltpu.VMEM((2, TOK, CW), BF16),
             pltpu.SemaphoreType.DMA((8,)),
-            pltpu.SemaphoreType.DMA((3, 2)),
-            pltpu.SemaphoreType.DMA((2, 2)),
+            pltpu.SemaphoreType.DMA((3, 8, 2)),
+            pltpu.SemaphoreType.DMA((2, 8, 2)),
             pltpu.SemaphoreType.DMA((16,)),
             pltpu.SemaphoreType.DMA((16,)),
             pltpu.SemaphoreType.DMA((15,)),
             pltpu.SemaphoreType.DMA((16,)),
+            pltpu.SemaphoreType.DMA((2,)),
+            pltpu.SemaphoreType.DMA((2,)),
+            pltpu.SemaphoreType.DMA((2,)),
         ],
         compiler_params=pltpu.CompilerParams(
             collective_id=0, has_side_effects=True, vmem_limit_bytes=VMEM_LIMIT
@@ -288,7 +342,7 @@
 def scan_kernel(
     x, pk, rout_hbm, bias_hbm, alog_hbm, skip_hbm,
     out,
-    dt, u, cum, cb, yl, pre, ha, hc, rw, bias, al, skip, bt, tot, pay, grp, xbuf, zbuf,
+    dt, u, cum, cb, yl, pre, ha, hc, rw, bias, al, skip, bt, tot, pay, pay_t, grp, grp_t, xbuf, xbuf_t, zbuf, zbuf_t,
     loc_sem, xs_sem, xr_sem, zs_sem, zr_sem,
 ):
     s = lax.axis_index("seq")
@@ -304,8 +358,8 @@
     ]
     for one in loads:
         one.start()
-    zbuf[...] = jnp.zeros_like(zbuf)
-    xbuf[...] = jnp.zeros_like(xbuf)
+    for one in (zbuf, zbuf_t, xbuf, xbuf_t):
+        one[...] = jnp.zeros_like(one)
     ha[...] = jnp.zeros_like(ha)
     hc[...] = jnp.zeros_like(hc)
 
@@ -371,10 +425,10 @@
                     yl[done, :] = dot(cb[done, :], ready[k])
                 for t in range(16):
                     for k in range(PAR):
-                        at_row = (p * PAR + k) * TOK + (2 * q + half) * 16 + t
-                        d = jnp.broadcast_to(dt[pl.ds(at_row, 1), :], (8, CW))
-                        w = jnp.broadcast_to(u[pl.ds(at_row, 1), :], (8, CW))
+                        near = pl.ds(pl.multiple_of((p * PAR + k) * TOK + q * 32, 32), 32)
                         lane = half * 16 + t
+                        d = jnp.broadcast_to(dt.at[near][lane: lane + 1, :], (8, CW))
+                        w = jnp.broadcast_to(u.at[near][lane: lane + 1, :], (8, CW))
                         for h in range(2):
                             b = jnp.broadcast_to(maps[k][8 * h: 8 * h + 8, lane: lane + 1], (8, TOK))
                             b = jnp.concatenate([b, b], axis=1)
@@ -405,55 +459,58 @@
         pre[seg] = state
         state = jnp.exp2(rate * t) * state + mine
         total = total + t
-    pay[pl.ds(0, NS), :] = state
-    pay[pl.ds(NS, 8), :] = jnp.broadcast_to(total, (8, CW))
+    pay[...] = state.astype(BF16)
+    pay_t[...] = total
     pl.semaphore_wait(barrier, 14)
 
-    sends = []
+    def xcopy(d, slot):
+        to = {"chan": chan(zi, xi + d)}
+        return [pltpu.make_async_remote_copy(
+            src_ref=o, dst_ref=i.at[slot], send_sem=xs_sem.at[d - 1, n], recv_sem=xr_sem.at[slot, n],
+            device_id=to, device_id_type=MESH)
+            for n, (o, i) in enumerate(((pay, xbuf), (pay_t, xbuf_t)))]
+
     for d in range(1, 4):
-        sends.append(pltpu.make_async_remote_copy(
-            src_ref=pay, dst_ref=xbuf.at[xi], send_sem=xs_sem.at[d - 1], recv_sem=xr_sem.at[xi],
-            device_id={"chan": chan(zi, xi + d)}, device_id_type=MESH))
-    for one in sends:
-        one.start()
+        for one in xcopy(d, xi):
+            one.start()
     for d in range(1, 4):
-        frm = lax.rem(xi + d, 4)
-        pltpu.make_async_remote_copy(
-            src_ref=pay, dst_ref=xbuf.at[frm], send_sem=xs_sem.at[d - 1], recv_sem=xr_sem.at[frm],
-            device_id={"chan": chan(zi, frm)}, device_id_type=MESH).wait_recv()
+        for one in xcopy(d, lax.rem(xi + d, 4)):
+            one.wait_recv()
     gs = jnp.zeros((NS, CW), F32)
     gt = jnp.zeros((1, CW), F32)
     ms = jnp.zeros((NS, CW), F32)
     mt = jnp.zeros((1, CW), F32)
-    own = pay[...]
     for i in range(4):
-        got = jnp.where(xi == i, own, xbuf[i])
-        os, ot = got[:NS], got[NS: NS + 1]
+        os = jnp.where(xi == i, state, xbuf[i].astype(F32))
+        ot = jnp.where(xi == i, total, xbuf_t[i])
         dec = jnp.exp2(rate * ot)
         gs = dec * gs + os
         gt = gt + ot
         ms = jnp.where(i < xi, gs, ms)
         mt = jnp.where(i < xi, gt, mt)
-    grp[pl.ds(0, NS), :] = gs
-    grp[pl.ds(NS, 8), :] = jnp.broadcast_to(gt, (8, CW))
+    grp[...] = gs.astype(BF16)
+    grp_t[...] = gt
 
     def zcopy(d, slot):
-        return pltpu.make_async_remote_copy(
-            src_ref=grp, dst_ref=zbuf.at[slot], send_sem=zs_sem.at[d], recv_sem=zr_sem.at[slot],
-            device_id={"chan": chan(zi + d, xi)}, device_id_type=MESH)
+        to = {"chan": chan(zi + d, xi)}
+        return [pltpu.make_async_remote_copy(
+            src_ref=o, dst_ref=i.at[slot], send_sem=zs_sem.at[d, n], recv_sem=zr_sem.at[slot, n],
+            device_id=to, device_id_type=MESH)
+            for n, (o, i) in enumerate(((grp, zbuf), (grp_t, zbuf_t)))]
 
     for d in range(11, 0, -1):
         @pl.when(zi + d < 12)
         def _():
-            zcopy(d, zi).start()
+            for one in zcopy(d, zi):
+                one.start()
     for d in range(1, 12):
         @pl.when(zi - d >= 0)
         def _():
-            zcopy(d, lax.rem(zi - d + 12, 12)).wait_recv()
+            for one in zcopy(d, lax.rem(zi - d + 12, 12)):
+                one.wait_recv()
     zs = jnp.zeros((NS, CW), F32)
     for i in range(11):
-        got = zbuf[i]
-        new = jnp.exp2(rate * got[NS: NS + 1]) * zs + got[:NS]
+        new = jnp.exp2(rate * zbuf_t[i]) * zs + zbuf[i].astype(F32)
         zs = jnp.where(i < zi, new, zs)
     row_in = jnp.exp2(rate * mt) * zs + ms
     done = jnp.zeros((1, CW), F32)
@@ -476,19 +533,22 @@
                 before = 32 * q
             write(pl.ds(pl.multiple_of(before, 16), 16), ready[0])
             for t in range(16):
-                d = jnp.broadcast_to(cum[pl.ds(32 * q + 16 * half + t, 1), :], (8, CW))
+                near = pl.ds(pl.multiple_of(32 * q, 32), 32)
+                d = jnp.broadcast_to(cum.at[near][16 * half + t: 16 * half + t + 1, :], (8, CW))
                 g = [jnp.exp2(d * rates[h]) * starts[h] for h in range(2)]
                 held[0, pl.ds(16 * t, 16), :] = jnp.concatenate(g, axis=0).astype(BF16)
         return 0
 
     lax.fori_loop(0, SEGS * TOK // 32, carried, 0)
     write(pl.ds(SEGS * TOK - 16, 16), hc[0])
-    for one in sends:
-        one.wait_send()
+    for d in range(1, 4):
+        for one in xcopy(d, xi):
+            one.wait_send()
     for d in range(1, 12):
         @pl.when(zi + d < 12)
         def _():
-            zcopy(d, zi).wait_send()
+            for one in zcopy(d, zi):
+                one.wait_send()
 
 
 def scan(x, pk, rank_out, dt_bias, a_log, skip_gain):
@@ -515,15 +575,19 @@
             pltpu.VMEM((1, CW), F32),
             pltpu.VMEM((SEGS * NS, TOK), F32),
             pltpu.VMEM((SEGS, CW), F32),
-            pltpu.VMEM((24, CW), F32),
-            pltpu.VMEM((24, CW), F32),
-            pltpu.VMEM((4, 24, CW), F32),
-            pltpu.VMEM((12, 24, CW), F32),
+            pltpu.VMEM((NS, CW), BF16),
+            pltpu.VMEM((1, CW), F32),
+            pltpu.VMEM((NS, CW), BF16),
+            pltpu.VMEM((1, CW), F32),
+            pltpu.VMEM((4, NS, CW), BF16),
+            pltpu.VMEM((4, 1, CW), F32),
+            pltpu.VMEM((12, NS, CW), BF16),
+            pltpu.VMEM((12, 1, CW), F32),
             pltpu.SemaphoreType.DMA((4,)),
-            pltpu.SemaphoreType.DMA((3,)),
-            pltpu.SemaphoreType.DMA((4,)),
-            pltpu.SemaphoreType.DMA((12,)),
-            pltpu.SemaphoreType.DMA((12,)),
+            pltpu.SemaphoreType.DMA((3, 2)),
+            pltpu.SemaphoreType.DMA((4, 2)),
+            pltpu.SemaphoreType.DMA((12, 2)),
+            pltpu.SemaphoreType.DMA((12, 2)),
         ],
         compiler_params=pltpu.CompilerParams(
             collective_id=1, has_side_effects=True, vmem_limit_bytes=VMEM_LIMIT

time: 112 us -> 99.3 us (0.89)
  the two profiles are of different devices: /device:TPU:513 before, /device:TPU:68 now
where the time goes in v1:
time: 99.3 us; the launch traced here: 99.1 us
  Pallas kernels  95.8 us (96%)
  local copies, waits for them, and re-layouts  2.57 us (3%)
    pallas_call x1, Pallas kernels, attend(): pl.pallas_call(attend_kernel, out_shape=(jax.ShapeDtypeStruct((1, TOK, 40...  54.2 us
    pallas_call x1, Pallas kernels, scan(): pl.pallas_call(scan_kernel, out_shape=jax.ShapeDtypeStruct((1, rows, CW),...  41.6 us
    unnamed x6, local copies, waits for them, and re-layouts  2.57 us

profile of v1, /device:TPU:68, one launch (start us, length us, event | category | flops | bytes accessed | tf_op | source)
XLA Modules:
  0.0 99.1 jit_solution(12074129278826710603)
XLA Ops:
  0.6 54.2 %attend.1 = (bf16[1,128,4096]{2,1,0:T(8,128)(2,1)}, bf16[2048,256]{1,0:T(8,128)(2,1)}, bf16[16,160,256]{2,1,0:T(8,128)(2,1)}) custom-call(s32[1,16]{1,0:T(1,128)} %doc.1, bf16[1,128,4096]{2,1,0:T(8,128)(2,1)} %q_hbm.1, bf16[1,128,1024]{2,1,0:T(8,128)(2,1)} %k_hbm.1, bf16[1,128,1024]{2,1,0:T(8,128)(2,1)} %v_hbm.1, bf16[4096,256]{1,0:T(8,128)(2,1)} %rin_hbm.1, ...), custom_call_target="tpu_custom_call" | custom-call | tf_op jit(solution)/shard_map/attend/pallas_call | solution.py:306
  54.8 0.0 copy-start.1
  54.8 41.6 %scan.1 = bf16[1,2048,256]{2,1,0:T(8,128)(2,1)} custom-call(bf16[2048,256]{1,0:T(8,128)(2,1)} %get-tuple-element.6.x, bf16[16,160,256]{2,1,0:T(8,128)(2,1)} %get-tuple-element.7.pk, bf16[256,4096]{1,0:T(8,128)(2,1)} %rout_hbm.1, f32[1,4096]{1,0:T(1,128)} %bitcast.6, f32[16,4096]{1,0:T(8,128)} %bitcast.5, f32[1,4096]{1,0:T(1,128)} %bitcast.7), custom_call_target="tpu_custom_call" | custom-call | tf_op jit(solution)/shard_map/scan/pallas_call | solution.py:558
  96.5 0.0 copy-done.1
  96.5 0.0 copy-start
  96.5 1.0 copy.14
  97.5 0.6 copy-done
  98.1 1.0 copy.15
Async XLA Ops:
  54.8 41.6 %copy-start.1 = (bf16[1,128,4096]{2,1,0:T(8,128)(2,1)S(1)}, bf16[1,128,4096]{2,1,0:T(8,128)(2,1)}, u32[]{:S(2)}) copy-start(bf16[1,128,4096]{2,1,0:T(8,128)(2,1)} %get-tuple-element.10) | copy-start | bytes 3145732
  96.5 1.6 %copy-start = (bf16[1,2048,256]{2,1,0:T(8,128)(2,1)S(1)}, bf16[1,2048,256]{2,1,0:T(8,128)(2,1)}, u32[]{:S(2)}) copy-start(bf16[1,2048,256]{2,1,0:T(8,128)(2,1)} %scan.1) | copy-start | bytes 3145732

commit v2 on v1

v2 whole, which is shorter than its diff:
```python
import functools
import math

import jax
import jax.numpy as jnp
from jax import lax
from jax.experimental import pallas as pl
from jax.experimental.pallas import tpu as pltpu
from jax.sharding import PartitionSpec as P

NS = 16
TOK = 128
SEGS = 16
PAR = 2
EARLY = 10
CW = 256
PACK = 160
ORDER = (7, 6, 1, 2, 5, 0, 3, 4)
LOG2E = 1.4426950408889634
MESH = pl.DeviceIdType.MESH
F32 = jnp.float32
BF16 = jnp.bfloat16
VMEM_LIMIT = 60 * 1024 * 1024


def dot(a, b, ca=1, cb=0):
    return lax.dot_general(a, b, (((ca,), (cb,)), ((), ())), preferred_element_type=F32)


def softplus(v):
    z = jnp.exp(-jnp.abs(v))
    series = z * (1.0 - z * (0.5 - z * (1.0 / 3.0 - z * 0.25)))
    return jnp.maximum(v, 0.0) + jnp.where(z < 0.03125, series, jnp.log(1.0 + z))


def row_kernel(
    doc, q_hbm, k_hbm, v_hbm, rin_hbm, bcw_hbm, rout_hbm, bias_hbm, alog_hbm, skip_hbm,
    attn_out, out,
    qb, kb, vb, wb, bb, ab, po, rb, x, pk,
    dt, u, cum, cb, yl, ebuf, pre, ha, hc, rw, bias, al, skip, bt, tot,
    pay, pay_t, grp, grp_t, xbuf, xbuf_t, zbuf, zbuf_t,
    loc_sem, kv_send, kv_recv, x_send, x_recv, p_send, p_recv, r_send, r_recv, f_send,
    xs_sem, xr_sem, zs_sem, zr_sem, ready,
):
    s = lax.axis_index("seq")
    y = lax.div(s, 2)
    c = lax.rem(s, 2)
    sib = s + 1 - 2 * c

    at = pl.multiple_of(s * CW, CW)

    def local(src, dst, i):
        return pltpu.make_async_copy(src, dst, loc_sem.at[i])

    def remote(src, dst, send, recv, to):
        return pltpu.make_async_remote_copy(
            src_ref=src, dst_ref=dst, send_sem=send, recv_sem=recv,
            device_id={"seq": to}, device_id_type=MESH,
        )

    loads = [
        local(k_hbm.at[0], kb.at[0], 0),
        local(q_hbm.at[0], qb, 1),
        local(v_hbm.at[0], vb.at[0], 2),
        local(rin_hbm, wb, 3),
        local(bcw_hbm, bb, 4),
        local(rout_hbm.at[:, pl.ds(at, CW)], rw, 8),
        local(bias_hbm.at[:, pl.ds(at, CW)], bias, 9),
        local(alog_hbm.at[:, pl.ds(at, CW)], al, 10),
        local(skip_hbm.at[:, pl.ds(at, CW)], skip, 11),
    ]
    r = lax.axis_index("chan")
    zi = lax.div(r, 4)
    xi = lax.rem(r, 4)

    def chan(zz, xx):
        return 4 * lax.rem(zz + 12, 12) + lax.rem(xx + 4, 4)

    for one in (zbuf, zbuf_t, xbuf, xbuf_t):
        one[...] = jnp.zeros_like(one)
    barrier = pltpu.get_barrier_semaphore()
    for d in range(1, 12):
        @pl.when(zi + d < 12)
        def _():
            pl.semaphore_signal(barrier, inc=1, device_id={"chan": chan(zi + d, xi)}, device_id_type=MESH)
    for d in range(1, 4):
        pl.semaphore_signal(barrier, inc=1, device_id={"chan": chan(zi, xi + d)}, device_id_type=MESH)
    for d in range(1, 16):
        pl.semaphore_signal(
            barrier, inc=1, device_id={"seq": lax.rem(s + d, 16)}, device_id_type=MESH
        )
    for one in loads:
        one.start()

    @pl.when(s < 1)
    def _():
        kb[1] = jnp.zeros_like(kb[1])
        vb[1] = jnp.zeros_like(vb[1])

    @pl.when(s < 2)
    def _():
        kb[2] = jnp.zeros_like(kb[2])
        vb[2] = jnp.zeros_like(vb[2])

    first = s * TOK
    qpos = first + lax.broadcasted_iota(jnp.int32, (TOK, TOK), 0)
    lane = lax.broadcasted_iota(jnp.int32, (TOK, TOK), 1)
    begin = jnp.zeros((TOK, TOK), jnp.int32)
    bound = jnp.int32(0)
    for j in range(16):
        bound = bound + doc[0, j]
        begin = jnp.where(qpos >= bound, bound, begin)
    masks = []
    for b in range(3):
        kpos = first - b * TOK + lane
        masks.append((kpos <= qpos) & (kpos >= begin))

    pl.semaphore_wait(barrier, 18 + zi)
    for d in range(1, 12):
        @pl.when(zi - d >= 0)
        def _():
            pl.semaphore_signal(ready, inc=1, device_id={"chan": chan(zi - d, xi)}, device_id_type=MESH)

    def group(chip, i):
        off = jnp.int32(0)
        for at, value in enumerate(ORDER):
            off = jnp.where(i == at, value, off)
        return lax.rem(chip + off, 8)

    to1 = lax.rem(s + 1, 16)
    to2 = lax.rem(s + 2, 16)
    both = ((k_hbm.at[0], kb), (v_hbm.at[0], vb))

    def head(chip, i):
        return pl.ds(pl.multiple_of(group(chip, i) * 128, 128), 128)

    def send1(i):
        cols = head(lax.div(to1, 2), i)
        return [remote(o.at[:, cols], d.at[1, :, cols], kv_send.at[0, i, n], kv_recv.at[0, i, n], to1)
                for n, (o, d) in enumerate(both)]

    def send2(i):
        cols = head(lax.div(to2, 2), i)
        return [remote(o.at[:, cols], d.at[2, :, cols], kv_send.at[1, i, n], kv_recv.at[1, i, n], to2)
                for n, (o, d) in enumerate(both)]

    def pass2(i):
        cols = head(y, i)
        return [remote(d.at[1, :, cols], d.at[2, :, cols], kv_send.at[2, i, n], kv_recv.at[1, i, n], sib)
                for n, (o, d) in enumerate(both)]

    def start_kv(i, _):
        for n in range(2):
            @pl.when(s < 15)
            def _():
                send1(i)[n].start()

            @pl.when((c == 0) & (s < 14))
            def _():
                send2(i)[n].start()

        return 0

    lax.fori_loop(0, 8, start_kv, 0)

    def arrive_kv(i):
        cols = head(y, i)
        for n, (o, d) in enumerate(both):
            @pl.when(s >= 1)
            def _():
                remote(d.at[0, :, cols], d.at[1, :, cols], kv_send.at[0, i, n], kv_recv.at[0, i, n], sib).wait_recv()

            @pl.when((c == 0) & (s >= 2))
            def _():
                pass2(i)[n].start()

        for n, (o, d) in enumerate(both):
            @pl.when(s >= 2)
            def _():
                remote(d.at[0, :, cols], d.at[2, :, cols], kv_send.at[1, i, n], kv_recv.at[1, i, n], sib).wait_recv()

    for one in loads[:3]:
        one.wait()

    def send_tiles(g):
        for cc in range(2):
            to = 2 * g + cc
            cols = pl.ds(pl.multiple_of(to * CW, CW), CW)
            here = pl.ds(pl.multiple_of(s * TOK, TOK), TOK)

            @pl.when(to != s)
            def _():
                remote(ab.at[:, cols], x.at[here], x_send.at[to], x_recv.at[s], to).start()

            @pl.when(to == s)
            def _():
                local(ab.at[:, cols], x.at[here], 5).start()

    scale = LOG2E / math.sqrt(128.0)

    def step(i, _):
        arrive_kv(i)
        g = group(y, i)
        qcols = pl.ds(pl.multiple_of(g * 512, 512), 512)
        kcols = pl.ds(pl.multiple_of(g * 128, 128), 128)
        keys = [kb[b, :, kcols] for b in range(3)]
        vals = [vb[b, :, kcols] for b in range(3)]
        for j in range(4):
            hcols = pl.ds(pl.multiple_of(g * 512 + j * 128, 128), 128)
            q = qb[:, hcols]
            t = [jnp.where(masks[b], dot(q, keys[b], 1, 1) * scale, -1e30) for b in range(3)]
            top = jnp.max(jnp.maximum(jnp.maximum(t[0], t[1]), t[2]), axis=1, keepdims=True)
            e = [jnp.exp2(one - top) for one in t]
            inv = 1.0 / jnp.sum(e[0] + e[1] + e[2], axis=1, keepdims=True)
            o = dot((e[0] * inv).astype(BF16), vals[0])
            o = o + dot((e[1] * inv).astype(BF16), vals[1])
            o = o + dot((e[2] * inv).astype(BF16), vals[2])
            ab[:, hcols] = o.astype(BF16)

        @pl.when((i > 0) & (i < 7))
        def _():
            send_tiles(group(y, i - 1))

        return 0

    lax.fori_loop(0, 8, step, 0)
    out_copy = local(ab, attn_out.at[0], 6)
    out_copy.start()

    loads[3].wait()
    loads[4].wait()
    toks = ab[...]
    po[pl.ds(0, TOK), :] = dot(toks, wb[...]).astype(BF16)
    bct = dot(bb[...], toks, 1, 1)
    po[pl.ds(TOK, 2 * NS), :] = jnp.concatenate([bct, bct], axis=1).astype(BF16)

    own = local(po, pk.at[s], 7)
    own.start()

    def slot(chip, core):
        return 2 * lax.rem(chip + 8, 8) + core

    right = slot(y + 1, c)
    left = slot(y - 1, c)
    ring = {}
    across = {}
    across[0] = remote(po, pk.at[s], p_send.at[7], p_recv.at[s], sib)
    ring[("r", 0)] = remote(po, pk.at[s], p_send.at[0], p_recv.at[s], right)
    ring[("l", 0)] = remote(po, pk.at[s], p_send.at[4], p_recv.at[s], left)
    ring[("r", 0)].start()
    ring[("l", 0)].start()
    across[0].start()

    def relay(cc):
        to = 2 * lax.rem(y + 4, 8) + cc
        cols = pl.ds(pl.multiple_of(to * CW, CW), CW)
        return remote(ab.at[:, cols], rb.at[cc], r_send.at[cc], r_recv.at[cc], left)

    def forward(cc):
        frm = slot(y + 1, c)
        here = pl.ds(pl.multiple_of(frm * TOK, TOK), TOK)
        to = 2 * lax.rem(y + 5, 8) + cc
        return remote(rb.at[cc], x.at[here], f_send.at[cc], x_recv.at[frm], to)

    for cc in range(2):
        relay(cc).start()

    for one in loads[5:]:
        one.wait()
    rate = -jnp.exp(al[...]) * LOG2E
    rates = (rate[:8], rate[8:])

    row = lax.broadcasted_iota(jnp.int32, (TOK, TOK), 0)
    col = lax.broadcasted_iota(jnp.int32, (TOK, TOK), 1)
    tri = (col <= row).astype(BF16)
    spread = (lax.rem(lax.broadcasted_iota(jnp.int32, (NS, CW), 1), NS)
              == lax.broadcasted_iota(jnp.int32, (NS, CW), 0)).astype(BF16)
    block = (lax.div(lax.broadcasted_iota(jnp.int32, (TOK, CW), 1), NS)
             == lax.rem(lax.broadcasted_iota(jnp.int32, (TOK, CW), 0), NS))

    def prepare(*segs):
        for seg in segs:
            rows = pl.ds(pl.multiple_of(seg * TOK, TOK), TOK)
            low = pk[seg, pl.ds(0, TOK), :]
            step = softplus(dot(low, rw[...]) + bias[...])
            dt[rows, :] = step
            hi = step.astype(BF16)
            lo = (step - hi.astype(F32)).astype(BF16)
            run = dot(tri, hi) + dot(tri, lo)
            cum[rows, :] = run
            tot[pl.ds(seg, 1), :] = run[TOK - 1:, :]
            maps = pk[seg, pl.ds(TOK, 2 * NS), pl.ds(0, TOK)]
            bt[pl.ds(pl.multiple_of(seg * NS, NS), NS), :] = maps[:NS].astype(F32)
            wide_c = dot(maps[NS:], spread, 0, 0)
            cb[rows, :] = jnp.where(block, wide_c, 0.0).astype(BF16)

    def arrived(at):
        remote(po, pk.at[at], p_send.at[0], p_recv.at[at], sib).wait_recv()

    for k in range(1, 5):
        far = slot(y - k, c)
        arrived(far)
        if k < 4:
            ring[("r", k)] = remote(pk.at[far], pk.at[far], p_send.at[k], p_recv.at[far], right)
            ring[("r", k)].start()
        across[k] = remote(pk.at[far], pk.at[far], p_send.at[7 + k], p_recv.at[far], sib)
        across[k].start()
        if k < 4:
            far = slot(y + k, c)
            arrived(far)
            if k < 3:
                ring[("l", k)] = remote(pk.at[far], pk.at[far], p_send.at[4 + k], p_recv.at[far], left)
                ring[("l", k)].start()
            across[-k] = remote(pk.at[far], pk.at[far], p_send.at[11 + k], p_recv.at[far], sib)
            across[-k].start()
        if k == 1:
            send_tiles(group(y, 6))
            for cc in range(2):
                relay(cc).wait_recv()
                forward(cc).start()
            own.wait()
            arrived(slot(y, 1 - c))
            prepare(s, sib)
        elif k < 4:
            for far in (slot(y - k + 1, 1 - c), slot(y + k - 1, 1 - c)):
                arrived(far)
            prepare(slot(y - k + 1, c), slot(y + k - 1, c))
            prepare(slot(y - k + 1, 1 - c), slot(y + k - 1, 1 - c))

    for k in (-3, 3, 4):
        arrived(slot(y + k, 1 - c))
    prepare(slot(y - 3, c), slot(y + 3, c))
    prepare(slot(y - 3, 1 - c), slot(y + 3, 1 - c))
    prepare(slot(y + 4, c), slot(y + 4, 1 - c))

    def tile(of):
        return remote(
            ab.at[:, pl.ds(0, CW)], x.at[pl.ds(0, TOK)], x_send.at[of], x_recv.at[of], of
        )

    local(ab.at[:, pl.ds(0, CW)], x.at[pl.ds(0, TOK)], 5).wait()
    for d in range(1, 16):
        tile(lax.rem(s + d, 16)).wait_recv()

    def drive(seg, _):
        rows = pl.ds(pl.multiple_of(seg * TOK, TOK), TOK)
        u[rows, :] = dt[rows, :] * x[rows, :].astype(F32)
        return 0

    lax.fori_loop(0, SEGS, drive, 0)
    ha[...] = jnp.zeros_like(ha)
    hc[...] = jnp.zeros_like(hc)

    def rows_of(seg, chunk):
        return pl.ds(pl.multiple_of(seg * TOK + chunk * 16, 16), 16)

    def pair(p, _):
        def body(q, carry):
            states, maps = carry
            states = [list(one) for one in states]
            for half, (held, ready) in enumerate(((ha, hc), (hc, ha)) * 2):
                for k in range(PAR):
                    if half == 0:
                        wrapped = q == 0
                        seg = jnp.where(wrapped, lax.rem(p + 7, 8), p) * PAR + k
                        done = rows_of(seg, jnp.where(wrapped, 7, 4 * q - 1))
                    else:
                        done = rows_of(p * PAR + k, 4 * q + half - 1)
                    yl[done, :] = dot(cb[done, :], ready[k])
                for t in range(16):
                    for k in range(PAR):
                        near = pl.ds(pl.multiple_of((p * PAR + k) * TOK + q * 64, 64), 64)
                        lane = half * 16 + t
                        d = jnp.broadcast_to(dt.at[near][lane: lane + 1, :], (8, CW))
                        w = jnp.broadcast_to(u.at[near][lane: lane + 1, :], (8, CW))
                        for h in range(2):
                            b = jnp.broadcast_to(maps[k][8 * h: 8 * h + 8, lane: lane + 1], (8, TOK))
                            b = jnp.concatenate([b, b], axis=1)
                            states[k][h] = jnp.exp2(d * rates[h]) * states[k][h] + w * b
                        held[k, pl.ds(16 * t, 16), :] = jnp.concatenate(states[k], axis=0).astype(BF16)
            maps = tuple(pltpu.roll(one, TOK - 64, axis=1) for one in maps)
            return tuple(tuple(one) for one in states), maps

        zero = jnp.zeros((8, CW), F32)
        maps = tuple(
            bt[pl.ds(pl.multiple_of((p * PAR + k) * NS, NS), NS), :] for k in range(PAR)
        )
        states, _ = lax.fori_loop(0, 2, body, (((zero, zero),) * PAR, maps))
        for k in range(PAR):
            pre[p * PAR + k] = jnp.concatenate(states[k], axis=0)
        return 0

    lax.fori_loop(0, SEGS // PAR, pair, 0)
    for k in range(PAR):
        done = rows_of(SEGS - PAR + k, 7)
        yl[done, :] = dot(cb[done, :], hc[k])

    state = jnp.zeros((NS, CW), F32)
    total = jnp.zeros((1, CW), F32)
    for seg in range(SEGS):
        mine = pre[seg]
        t = tot[pl.ds(seg, 1), :]
        pre[seg] = state
        state = jnp.exp2(rate * t) * state + mine
        total = total + t
    pay[...] = state.astype(BF16)
    pay_t[...] = total

    def xcopy(d, slot):
        to = {"chan": chan(zi, xi + d)}
        return [pltpu.make_async_remote_copy(
            src_ref=o, dst_ref=i.at[slot], send_sem=xs_sem.at[d - 1, n], recv_sem=xr_sem.at[slot, n],
            device_id=to, device_id_type=MESH)
            for n, (o, i) in enumerate(((pay, xbuf), (pay_t, xbuf_t)))]

    for d in range(1, 4):
        for one in xcopy(d, xi):
            one.start()

    def decay(q, _):
        near = pl.ds(pl.multiple_of(64 * q, 64), 64)
        for t in range(64):
            d = jnp.broadcast_to(cum.at[near][t: t + 1, :], (8, CW))
            e = [jnp.exp2(d * rates[h]).astype(BF16) for h in range(2)]
            held = pl.ds(pl.multiple_of(1024 * q + 16 * t, 16), 16)
            ebuf[held, :] = jnp.concatenate(e, axis=0)
        return 0

    lax.fori_loop(0, EARLY, decay, 0)
    for d in range(1, 4):
        for one in xcopy(d, lax.rem(xi + d, 4)):
            one.wait_recv()
    gs = jnp.zeros((NS, CW), F32)
    gt = jnp.zeros((1, CW), F32)
    ms = jnp.zeros((NS, CW), F32)
    mt = jnp.zeros((1, CW), F32)
    for i in range(4):
        os = jnp.where(xi == i, state, xbuf[i].astype(F32))
        ot = jnp.where(xi == i, total, xbuf_t[i])
        dec = jnp.exp2(rate * ot)
        gs = dec * gs + os
        gt = gt + ot
        ms = jnp.where(i < xi, gs, ms)
        mt = jnp.where(i < xi, gt, mt)
    grp[...] = gs.astype(BF16)
    grp_t[...] = gt

    def zcopy(d, slot):
        to = {"chan": chan(zi + d, xi)}
        return [pltpu.make_async_remote_copy(
            src_ref=o, dst_ref=i.at[slot], send_sem=zs_sem.at[d, n], recv_sem=zr_sem.at[slot, n],
            device_id=to, device_id_type=MESH)
            for n, (o, i) in enumerate(((grp, zbuf), (grp_t, zbuf_t)))]


    @pl.when(zi < 11)
    def _():
        pl.semaphore_wait(ready, 11 - zi)

    for d in range(11, 0, -1):
        @pl.when(zi + d < 12)
        def _():
            for one in zcopy(d, zi):
                one.start()
    lax.fori_loop(EARLY, SEGS * TOK // 64, decay, 0)
    for d in range(1, 12):
        @pl.when(zi - d >= 0)
        def _():
            for one in zcopy(d, lax.rem(zi - d + 12, 12)):
                one.wait_recv()
    zs = jnp.zeros((NS, CW), F32)
    for i in range(11):
        new = jnp.exp2(rate * zbuf_t[i]) * zs + zbuf[i].astype(F32)
        zs = jnp.where(i < zi, new, zs)
    row_in = jnp.exp2(rate * mt) * zs + ms
    done = jnp.zeros((1, CW), F32)
    for seg in range(SEGS):
        pre[seg] = pre[seg] + jnp.exp2(rate * done) * row_in
        done = done + tot[pl.ds(seg, 1), :]

    def carried(q, _):
        start = pre[q].astype(BF16)
        starts = jnp.concatenate([start] * 16, axis=0)
        for j in range(8):
            rows = pl.ds(pl.multiple_of(TOK * q + 16 * j, 16), 16)
            held = pl.ds(pl.multiple_of(NS * TOK * q + 256 * j, 256), 256)
            got = yl[rows, :] + dot(cb[rows, :], ebuf[held, :] * starts)
            out[0, rows, :] = (got + skip[...] * x[rows, :].astype(F32)).astype(BF16)
        return 0

    lax.fori_loop(0, SEGS, carried, 0)
    out_copy.wait()
    for one in list(ring.values()) + list(across.values()):
        one.wait_send()
    for cc in range(2):
        relay(cc).wait_send()
        forward(cc).wait_send()

    def end_kv(i, _):
        for n in range(2):
            @pl.when(s < 15)
            def _():
                send1(i)[n].wait_send()

            @pl.when((c == 0) & (s < 14))
            def _():
                send2(i)[n].wait_send()

            @pl.when((c == 0) & (s >= 2))
            def _():
                pass2(i)[n].wait_send()

        return 0

    lax.fori_loop(0, 8, end_kv, 0)
    for d in range(1, 16):
        to = lax.rem(s + d, 16)

        @pl.when(lax.rem(lax.div(to, 2) + 8 - y, 8) != 4)
        def _():
            tile(to).wait_send()

    for d in range(1, 4):
        for one in xcopy(d, xi):
            one.wait_send()
    for d in range(1, 12):
        @pl.when(zi + d < 12)
        def _():
            for one in zcopy(d, zi):
                one.wait_send()


def row(doc, queries, keys, values, rank_in, bc_weight, rank_out, dt_bias, a_log, skip_gain):
    anyspace = pl.BlockSpec(memory_space=pl.ANY)
    rows = SEGS * TOK
    return pl.pallas_call(
        row_kernel,
        out_shape=(
            jax.ShapeDtypeStruct((1, TOK, 4096), BF16),
            jax.ShapeDtypeStruct((1, rows, CW), BF16),
        ),
        in_specs=[pl.BlockSpec(memory_space=pltpu.SMEM)] + [anyspace] * 9,
        out_specs=(anyspace, pl.BlockSpec(memory_space=pltpu.VMEM)),
        scratch_shapes=[
            pltpu.VMEM((TOK, 4096), BF16),
            pltpu.VMEM((3, TOK, 1024), BF16),
            pltpu.VMEM((3, TOK, 1024), BF16),
            pltpu.VMEM((4096, 256), BF16),
            pltpu.VMEM((2 * NS, 4096), BF16),
            pltpu.VMEM((TOK, 4096), BF16),
            pltpu.VMEM((PACK, CW), BF16),
            pltpu.VMEM((2, TOK, CW), BF16),
            pltpu.VMEM((rows, CW), BF16),
            pltpu.VMEM((SEGS, PACK, CW), BF16),
            pltpu.VMEM((rows, CW), F32),
            pltpu.VMEM((rows, CW), F32),
            pltpu.VMEM((rows, CW), F32),
            pltpu.VMEM((rows, CW), BF16),
            pltpu.VMEM((rows, CW), F32),
            pltpu.VMEM((rows * NS, CW), BF16),
            pltpu.VMEM((SEGS, NS, CW), F32),
            pltpu.VMEM((PAR, 256, CW), BF16),
            pltpu.VMEM((PAR, 256, CW), BF16),
            pltpu.VMEM((256, CW), BF16),
            pltpu.VMEM((1, CW), F32),
            pltpu.VMEM((NS, CW), F32),
            pltpu.VMEM((1, CW), F32),
            pltpu.VMEM((SEGS * NS, TOK), F32),
            pltpu.VMEM((SEGS, CW), F32),
            pltpu.VMEM((NS, CW), BF16),
            pltpu.VMEM((1, CW), F32),
            pltpu.VMEM((NS, CW), BF16),
            pltpu.VMEM((1, CW), F32),
            pltpu.VMEM((4, NS, CW), BF16),
            pltpu.VMEM((4, 1, CW), F32),
            pltpu.VMEM((12, NS, CW), BF16),
            pltpu.VMEM((12, 1, CW), F32),
            pltpu.SemaphoreType.DMA((12,)),
            pltpu.SemaphoreType.DMA((3, 8, 2)),
            pltpu.SemaphoreType.DMA((2, 8, 2)),
            pltpu.SemaphoreType.DMA((16,)),
            pltpu.SemaphoreType.DMA((16,)),
            pltpu.SemaphoreType.DMA((15,)),
            pltpu.SemaphoreType.DMA((16,)),
            pltpu.SemaphoreType.DMA((2,)),
            pltpu.SemaphoreType.DMA((2,)),
            pltpu.SemaphoreType.DMA((2,)),
            pltpu.SemaphoreType.DMA((3, 2)),
            pltpu.SemaphoreType.DMA((4, 2)),
            pltpu.SemaphoreType.DMA((12, 2)),
            pltpu.SemaphoreType.DMA((12, 2)),
            pltpu.SemaphoreType.REGULAR,
        ],
        compiler_params=pltpu.CompilerParams(
            collective_id=0, has_side_effects=True, vmem_limit_bytes=VMEM_LIMIT
        ),
        name="row",
    )(doc, queries, keys, values, rank_in, bc_weight, rank_out, dt_bias, a_log, skip_gain)


def local(
    queries, keys, values, doc_lengths, rank_in, bc_weight, rank_out, dt_bias, a_log, skip_gain
):
    return row(
        doc_lengths, queries, keys, values, rank_in, bc_weight.T,
        rank_out, dt_bias[None], a_log.T, skip_gain[None],
    )


def solution(mesh):
    return jax.shard_map(
        local,
        mesh=mesh,
        in_specs=(
            P("chan", "seq", None),
            P("chan", "seq", None),
            P("chan", "seq", None),
            P("chan", None),
            P(),
            P(),
            P(),
            P(),
            P(),
            P(),
        ),
        out_specs=(P("chan", "seq", None), P("chan", None, "seq")),
        check_vma=False,
    )
```

time: 99.3 us -> 85.5 us (0.86)
  the two profiles are of different devices: /device:TPU:68 before, /device:TPU:56 now
where the time goes in v2:
time: 85.5 us; the launch traced here: 85.3 us
  Pallas kernels  81.3 us (95%)
  local copies, waits for them, and re-layouts  3.35 us (4%)
    pallas_call x1, Pallas kernels, row(): pl.pallas_call(row_kernel, out_shape=(jax.ShapeDtypeStruct((1, TOK, 4096)...  81.3 us
    unnamed x4, local copies, waits for them, and re-layouts  3.35 us

profile of v2, /device:TPU:56, one launch (start us, length us, event | category | flops | bytes accessed | tf_op | source)
XLA Modules:
  0.0 85.3 jit_solution(7686637935494591388)
XLA Ops:
  0.6 81.3 %row.1 = (bf16[1,128,4096]{2,1,0:T(8,128)(2,1)}, bf16[1,2048,256]{2,1,0:T(8,128)(2,1)}) custom-call(s32[1,16]{1,0:T(1,128)} %doc.1, bf16[1,128,4096]{2,1,0:T(8,128)(2,1)} %q_hbm.1, bf16[1,128,1024]{2,1,0:T(8,128)(2,1)} %k_hbm.1, bf16[1,128,1024]{2,1,0:T(8,128)(2,1)} %v_hbm.1, bf16[4096,256]{1,0:T(8,128)(2,1)} %rin_hbm.1, bf16[32,4096]{1,0:T(8,128)(2,1)} %bitcast.4, ...), custom_call_target="tpu_custom_call" | custom-call | tf_op jit(solution)/shard_map/row/pallas_call | solution.py:536
  81.9 0.0 copy-start
  82.0 2.4 %copy.14 = bf16[1,128,4096]{2,1,0:T(8,128)(2,1)} copy(bf16[1,128,4096]{2,1,0:T(8,128)(2,1)} %get-tuple-element.4) | data formatting | bytes 2097152
  84.3 0.0 copy-done
  84.3 1.0 %copy.15 = bf16[1,2048,256]{2,1,0:T(8,128)(2,1)} copy(bf16[1,2048,256]{2,1,0:T(8,128)(2,1)S(1)} %copy-done) | data formatting | bytes 2097152
Async XLA Ops:
  81.9 2.4 %copy-start = (bf16[1,2048,256]{2,1,0:T(8,128)(2,1)S(1)}, bf16[1,2048,256]{2,1,0:T(8,128)(2,1)}, u32[]{:S(2)}) copy-start(bf16[1,2048,256]{2,1,0:T(8,128)(2,1)} %get-tuple-element.5) | copy-start | bytes 3145732

commit v3 on v2

--- a/solution.py
+++ b/solution.py
@@ -12,7 +12,7 @@
 TOK = 128
 SEGS = 16
 PAR = 2
-EARLY = 10
+EARLY = 5
 CW = 256
 PACK = 160
 ORDER = (7, 6, 1, 2, 5, 0, 3, 4)
@@ -40,7 +40,7 @@
     dt, u, cum, cb, yl, ebuf, pre, ha, hc, rw, bias, al, skip, bt, tot,
     pay, pay_t, grp, grp_t, xbuf, xbuf_t, zbuf, zbuf_t,
     loc_sem, kv_send, kv_recv, x_send, x_recv, p_send, p_recv, r_send, r_recv, f_send,
-    xs_sem, xr_sem, zs_sem, zr_sem, ready,
+    xs_sem, xr_sem, zs_sem, zr_sem, ready, ready_x,
 ):
     s = lax.axis_index("seq")
     y = lax.div(s, 2)
@@ -84,7 +84,9 @@
         def _():
             pl.semaphore_signal(barrier, inc=1, device_id={"chan": chan(zi + d, xi)}, device_id_type=MESH)
     for d in range(1, 4):
-        pl.semaphore_signal(barrier, inc=1, device_id={"chan": chan(zi, xi + d)}, device_id_type=MESH)
+        @pl.when(xi + d < 4)
+        def _():
+            pl.semaphore_signal(barrier, inc=1, device_id={"chan": chan(zi, xi + d)}, device_id_type=MESH)
     for d in range(1, 16):
         pl.semaphore_signal(
             barrier, inc=1, device_id={"seq": lax.rem(s + d, 16)}, device_id_type=MESH
@@ -115,7 +117,11 @@
         kpos = first - b * TOK + lane
         masks.append((kpos <= qpos) & (kpos >= begin))
 
-    pl.semaphore_wait(barrier, 18 + zi)
+    pl.semaphore_wait(barrier, 15 + zi + xi)
+    for d in range(1, 4):
+        @pl.when(xi - d >= 0)
+        def _():
+            pl.semaphore_signal(ready_x, inc=1, device_id={"chan": chan(zi, xi - d)}, device_id_type=MESH)
     for d in range(1, 12):
         @pl.when(zi - d >= 0)
         def _():
@@ -413,16 +419,20 @@
             device_id=to, device_id_type=MESH)
             for n, (o, i) in enumerate(((pay, xbuf), (pay_t, xbuf_t)))]
 
+    @pl.when(xi < 3)
+    def _():
+        pl.semaphore_wait(ready_x, 3 - xi)
+
     for d in range(1, 4):
         for one in xcopy(d, xi):
             one.start()
 
     def decay(q, _):
-        near = pl.ds(pl.multiple_of(64 * q, 64), 64)
-        for t in range(64):
+        near = pl.ds(pl.multiple_of(TOK * q, TOK), TOK)
+        for t in range(TOK):
             d = jnp.broadcast_to(cum.at[near][t: t + 1, :], (8, CW))
             e = [jnp.exp2(d * rates[h]).astype(BF16) for h in range(2)]
-            held = pl.ds(pl.multiple_of(1024 * q + 16 * t, 16), 16)
+            held = pl.ds(pl.multiple_of(NS * TOK * q + 16 * t, 16), 16)
             ebuf[held, :] = jnp.concatenate(e, axis=0)
         return 0
 
@@ -462,7 +472,7 @@
         def _():
             for one in zcopy(d, zi):
                 one.start()
-    lax.fori_loop(EARLY, SEGS * TOK // 64, decay, 0)
+    lax.fori_loop(EARLY, SEGS, decay, 0)
     for d in range(1, 12):
         @pl.when(zi - d >= 0)
         def _():
@@ -590,6 +600,7 @@
             pltpu.SemaphoreType.DMA((12, 2)),
             pltpu.SemaphoreType.DMA((12, 2)),
             pltpu.SemaphoreType.REGULAR,
+            pltpu.SemaphoreType.REGULAR,
         ],
         compiler_params=pltpu.CompilerParams(
             collective_id=0, has_side_effects=True, vmem_limit_bytes=VMEM_LIMIT

time: 85.5 us -> 85.4 us (level)
  no operation moved by 1% of the time
where the time goes in v3:
time: 85.4 us; the launch traced here: 85.2 us
  Pallas kernels  81.2 us (95%)
  local copies, waits for them, and re-layouts  3.35 us (4%)
    pallas_call x1, Pallas kernels, row(): pl.pallas_call(row_kernel, out_shape=(jax.ShapeDtypeStruct((1, TOK, 4096)...  81.2 us
    unnamed x4, local copies, waits for them, and re-layouts  3.35 us

profile of v3, /device:TPU:56, one launch (start us, length us, event | category | flops | bytes accessed | tf_op | source)
XLA Modules:
  0.0 85.2 jit_solution(10834359500209395270)
XLA Ops:
  0.6 81.2 %row.1 = (bf16[1,128,4096]{2,1,0:T(8,128)(2,1)}, bf16[1,2048,256]{2,1,0:T(8,128)(2,1)}) custom-call(s32[1,16]{1,0:T(1,128)} %doc.1, bf16[1,128,4096]{2,1,0:T(8,128)(2,1)} %q_hbm.1, bf16[1,128,1024]{2,1,0:T(8,128)(2,1)} %k_hbm.1, bf16[1,128,1024]{2,1,0:T(8,128)(2,1)} %v_hbm.1, bf16[4096,256]{1,0:T(8,128)(2,1)} %rin_hbm.1, bf16[32,4096]{1,0:T(8,128)(2,1)} %bitcast.4, ...), custom_call_target="tpu_custom_call" | custom-call | tf_op jit(solution)/shard_map/row/pallas_call | solution.py:546
  81.9 0.0 copy-start
  81.9 2.4 %copy.14 = bf16[1,128,4096]{2,1,0:T(8,128)(2,1)} copy(bf16[1,128,4096]{2,1,0:T(8,128)(2,1)} %get-tuple-element.4) | data formatting | bytes 2097152
  84.3 0.0 copy-done
  84.3 1.0 %copy.15 = bf16[1,2048,256]{2,1,0:T(8,128)(2,1)} copy(bf16[1,2048,256]{2,1,0:T(8,128)(2,1)S(1)} %copy-done) | data formatting | bytes 2097152
Async XLA Ops:
  81.9 2.4 %copy-start = (bf16[1,2048,256]{2,1,0:T(8,128)(2,1)S(1)}, bf16[1,2048,256]{2,1,0:T(8,128)(2,1)}, u32[]{:S(2)}) copy-start(bf16[1,2048,256]{2,1,0:T(8,128)(2,1)} %get-tuple-element.5) | copy-start | bytes 3145732
